TPU v7x, 512 devices: a whole 4x8x8 slice. The times are simulated.
512 devices in a mesh: req: 128 (over z, y, core), tp: 4 (over x).
Axes of the slice: x: 4, y: 8, z: 8, core: 2. Of those that a mesh axis runs over, the one named last changes fastest.
Arguments:
- tokens: bfloat16 [49152, 3200], P('req'), may hold values from -6 to 6
- norm_gain: float32 [3200], replicated, may hold values from 0.5 to 2
- w_qkv: bfloat16 [3200, 6144], P('req', 'tp'), may hold values from -1 to 1
- q_gain: float32 [2048], P('tp'), may hold values from 0.5 to 2.5
- k_gain: float32 [2048], P('tp'), may hold values from 0.5 to 2.5
- w_out: bfloat16 [2048, 3200], P('tp', 'req'), may hold values from -0.125 to 0.125
- grids: int32 [384, 2], P('req'), may hold values from 2 to 16, as said below
- owners: int32 [12288], P('req'), may hold values from 0 to 127, as said below
- proj_gain: float32 [4, 3200], P(None, 'tp'), may hold values from 0.5 to 2
- proj_bias: float32 [4, 3200], P(None, 'tp'), may hold values from -3 to 3
Outputs:
- received: bfloat16 [32768, 4, 3200], P('req', None, 'tp')
Inputs may be any that keep to these rules, and one draw needn't show every extreme that they name: `grids`: each image spans at least 2 half grid rows. The images of one device together take at most 96 merged slots, and on one device in every draw exactly 96. `owners`: no device's merged slots, live or padding, name one owner more than 2 times; in every draw one owner is named exactly 2 times by every device.
All inputs are finite; a program needn't handle non-finite values.
Results may differ from a plain program's by a relative error of at most 0.009.
Values may be sent and summed in bfloat16 or wider, within the bound.
A program may use at most 128 MiB of HBM per device.

v0:
```python
import math
import jax
import jax.numpy as jnp
from jax import lax
from jax.sharding import PartitionSpec as P

D = 3200
HEADS = 16
HEAD_DIM = 128


def from_everyone(x, axis):
    copies = jnp.broadcast_to(x, (lax.axis_size(axis), *x.shape))
    return lax.all_to_all(copies, axis, split_axis=0, concat_axis=0, tiled=True)


def over_copies(x, axis):
    everything = from_everyone(x, axis)
    return jnp.sum(everything, axis=0)


def in_one(arrays, axis):
    ravelled, at, done = (jnp.concatenate([a.reshape(-1) for a in arrays]), 0, [])
    subtotal = over_copies(ravelled, axis)
    for a in arrays:
        done.append(subtotal[at : at + a.size].reshape(a.shape))
        at += a.size
    return tuple(done)


def merge_layout(grid, token_count, slot_count):
    half_rows = grid[:, 0]
    half_cols = grid[:, 1]
    image_slots = half_rows * half_cols
    slot_ends = jnp.cumsum(image_slots)
    slot_starts = slot_ends - image_slots
    slot_ids = jnp.arange(slot_count, dtype=jnp.int32)
    image_ids = jnp.sum((slot_ids[:, None] >= slot_ends[None, :]).astype(jnp.int32), axis=1)
    image_count = grid.shape[0]
    is_live = image_ids < image_count
    one_hot = (image_ids[:, None] == jnp.arange(image_count, dtype=jnp.int32)[None, :]).astype(
        jnp.int32
    )
    cols_here = jnp.maximum(jnp.sum(one_hot * half_cols[None, :], axis=1), 1)
    start_here = jnp.sum(one_hot * slot_starts[None, :], axis=1)
    offset = slot_ids - start_here
    row_half = offset // cols_here
    col_half = offset % cols_here
    first_row = 4 * start_here + 4 * row_half * cols_here + 2 * col_half
    patch_rows = jnp.stack(
        [first_row, first_row + 1, first_row + 2 * cols_here, first_row + 2 * cols_here + 1], axis=1
    )
    patch_rows = jnp.where(is_live[:, None], patch_rows, 0)
    token_ids = jnp.arange(token_count, dtype=jnp.int32)
    segment = jnp.sum((token_ids[:, None] >= 4 * slot_ends[None, :]).astype(jnp.int32), axis=1)
    return (patch_rows, is_live, segment)


def owner_ranks(owner_ids, is_live):
    slot_ids = jnp.arange(owner_ids.shape[0], dtype=jnp.int32)
    earlier = (
        (owner_ids[:, None] == owner_ids[None, :])
        & (slot_ids[None, :] < slot_ids[:, None])
        & is_live[None, :]
    )
    return jnp.sum(earlier.astype(jnp.int32), axis=1)


def body(tokens, norm_gain, w_qkv, q_gain, k_gain, w_out, grids, owners, proj_gain, proj_bias):
    token_count = tokens.shape[0]
    slot_count = owners.shape[0]
    quarter = proj_gain.shape[1]
    head_share = q_gain.shape[0]
    head_count = head_share // HEAD_DIM
    head_width = HEADS * HEAD_DIM
    score_scale = 1.0 / math.sqrt(HEAD_DIM)
    feature_total = 4 * D
    devices_req = lax.axis_size("req")
    capacity = max(2, (2 * slot_count + devices_req - 1) // devices_req)
    patch_rows, is_live, segment = merge_layout(grids, token_count, slot_count)
    token_float = tokens.astype(jnp.float32)
    mean_square = jnp.mean(token_float * token_float, axis=1, keepdims=True)
    normed = (token_float * lax.rsqrt(mean_square + 1e-06) * norm_gain).astype(jnp.bfloat16)
    projected = jnp.dot(
        normed, lax.all_gather(w_qkv, "req", axis=0, tiled=True), preferred_element_type=jnp.float32
    )
    projected = projected.reshape(token_count, head_count, 3, HEAD_DIM)
    queries = projected[:, :, 0]
    key_vecs = projected[:, :, 1]
    values = projected[:, :, 2].astype(jnp.bfloat16)
    q_gains = q_gain.reshape(head_count, HEAD_DIM)
    k_gains = k_gain.reshape(head_count, HEAD_DIM)
    local_q = jnp.sum(queries * queries, axis=(1, 2))
    local_k = jnp.sum(key_vecs * key_vecs, axis=(1, 2))
    q_total, k_total = in_one((local_q, local_k), "tp")
    q_scale = lax.rsqrt(q_total / head_width + 1e-06)
    k_scale = lax.rsqrt(k_total / head_width + 1e-06)
    q_normed = queries * q_scale[:, None, None] * q_gains
    k_normed = key_vecs * k_scale[:, None, None] * k_gains
    scores = (
        jnp.einsum("qhd,khd->hqk", q_normed, k_normed, precision=lax.Precision.HIGHEST)
        * score_scale
    )
    same_image = segment[:, None] == segment[None, :]
    scores = jnp.where(same_image[None], scores, -1e30)
    row_top = jnp.max(scores, axis=2, keepdims=True)
    weights_raw = jnp.exp(scores - row_top)
    probs = (weights_raw / jnp.sum(weights_raw, axis=2, keepdims=True)).astype(jnp.bfloat16)
    attended = jnp.einsum("hqk,khd->qhd", probs, values, preferred_element_type=jnp.float32)
    attended = attended.astype(jnp.bfloat16).reshape(token_count, head_share)
    partial_sum = jnp.dot(
        attended,
        lax.all_gather(w_out, "req", axis=1, tiled=True),
        preferred_element_type=jnp.float32,
    )
    mine = lax.psum_scatter(
        partial_sum.astype(jnp.bfloat16), "tp", scatter_dimension=1, tiled=True
    ).astype(jnp.float32)
    token_mine = lax.dynamic_slice_in_dim(token_float, lax.axis_index("tp") * quarter, quarter, 1)
    hidden = (token_mine + mine).astype(jnp.bfloat16)
    merged = jnp.where(is_live[:, None, None], hidden[patch_rows], jnp.zeros((), jnp.bfloat16))
    ranks = owner_ranks(owners, is_live)
    target_owner = jnp.where(is_live, owners, devices_req)
    merged_float = merged.astype(jnp.float32)
    row_sum = jnp.sum(merged_float, axis=(1, 2))
    row_sq = jnp.sum(merged_float * merged_float, axis=(1, 2))
    row_sum, row_sq = in_one((row_sum, row_sq), "tp")
    mean_value = row_sum / feature_total
    variance = row_sq / feature_total - mean_value * mean_value
    normed_rows = (merged_float - mean_value[:, None, None]) * lax.rsqrt(variance + 1e-05)[
        :, None, None
    ] * proj_gain + proj_bias
    normed_rows = jnp.where(is_live[:, None, None], normed_rows, 0.0).astype(jnp.bfloat16)
    send_slots = jnp.zeros((devices_req, capacity, 4, quarter), jnp.bfloat16)
    send_slots = send_slots.at[target_owner, ranks].set(normed_rows, mode="drop")
    arrived = lax.all_to_all(send_slots, "req", split_axis=0, concat_axis=0, tiled=True)
    result = arrived.reshape(devices_req * capacity, 4, quarter)
    return result


def solution(mesh):
    placed = (
        P("req", None),
        P(),
        P("req", "tp"),
        P("tp"),
        P("tp"),
        P("tp", "req"),
        P("req", None),
        P("req"),
        P(None, "tp"),
        P(None, "tp"),
    )
    return jax.shard_map(
        body, mesh=mesh, in_specs=placed, out_specs=P("req", None, "tp"), check_vma=False
    )
```

profile of v0, /device:TPU:8, one launch (start us, length us, event | category | flops | bytes accessed | tf_op | source)
XLA Modules:
  0.0 339.7 jit_solution(6515635948324033190)
XLA Ops:
  6.5 0.0 all-gather.5.cloned.1.call-start
  6.5 0.7 all-gather.5.cloned.1.call-update
  7.3 0.0 all-gather.7.cloned.1.call-start
  7.3 0.7 all-gather.7.cloned.1.call-update
  8.0 0.0 copy-start.5
  8.0 4.2 %copy.44 = bf16[384,3200]{0,1:T(8,128)(2,1)S(1)} copy(bf16[384,3200]{1,0:T(8,128)(2,1)} %param.10) | data formatting | bytes 4915200 | tf_op args[0]
  12.3 0.0 copy-done.5
  12.3 0.2 reduce-window.7
  12.5 0.1 convert_reduce_fusion.2
  12.5 0.6 multiply_reduce_fusion
  13.2 92.8 %all-gather.5.cloned.1.call-done = bf16[128,25,1536]{2,1,0:T(8,128)(2,1)} async-done(((bf16[1,25,1536]{2,1,0:T(8,128)(2,1)}), bf16[128,25,1536]{2,1,0:T(8,128)(2,1)}) %all-gather.5.cloned.1.call-update) | async-done | bytes 9830416 | tf_op jit(solution)/shard_map/all_gather | solution.py:85
  105.9 14.4 %reshape.394 = bf16[3200,1536]{1,0:T(8,128)(2,1)} reshape(bf16[128,25,1536]{2,1,0:T(8,128)(2,1)} %all-gather.5.cloned.1.call-done) | data formatting | bytes 19660800
  120.3 0.0 copy-done.8
  120.3 8.5 %fusion.1 = f32[384,1536]{0,1:T(8,128)S(1)} fusion(bf16[3200,1536]{1,0:T(8,128)(2,1)} %reshape.394, f32[3200]{0:T(1024)S(1)} %copy-done.8, f32[384]{0:T(512)S(1)} %add_rsqrt_fusion.2, bf16[384,3200]{0,1:T(8,128)(2,1)S(1)} %copy.44), kind=kOutput, calls=%fused_computation.6 | convolution fusion | flops 3779788800 | bytes 14661632 | tf_op jit(solution)/shard_map/dot_general | solution.py:84
  128.8 0.0 copy-start
  128.8 1.4 copy-done
  130.2 0.1 multiply_reduce_fusion.2
  130.4 0.6 broadcast_in_dim.61
  131.0 4.2 %all-to-all-start = ((f32[4,1,768]{2,1,0:T(1,128)}), f32[4,1,768]{2,1,0:T(1,128)S(1)}, u32[]{:S(2)}, u32[]{:S(2)}) async-start(f32[4,1,768]{2,1,0:T(1,128)} %broadcast_in_dim.61), calls=%async_computation | async-start | bytes 24576 | tf_op jit(solution)/shard_map/all_to_all | solution.py:14
  135.2 0.0 reduce-scatter.2.cloned.1.call-start
  135.2 0.1 broadcast_compare_fusion
  135.4 0.0 copy-start.6
  135.4 0.0 copy-start.7
  135.4 54.9 %all-gather.7.cloned.1.call-done = bf16[128,25,512]{2,1,0:T(8,128)(2,1)} async-done(((bf16[1,25,512]{2,1,0:T(8,128)(2,1)}), bf16[128,25,512]{2,1,0:T(8,128)(2,1)}) %all-gather.7.cloned.1.call-update) | async-done | bytes 3276816 | tf_op jit(solution)/shard_map/all_gather | solution.py:113
  190.3 5.8 %reshape.396 = bf16[3200,512]{1,0:T(8,128)(2,1)} reshape(bf16[128,25,512]{2,1,0:T(8,128)(2,1)} %all-gather.7.cloned.1.call-done) | data formatting | bytes 6553600
  196.1 0.0 all-to-all-done
  196.1 0.0 copy-done.6
  196.1 0.0 copy-done.7
  196.2 3.7 %fusion.15 = f32[4,384,384]{1,2,0:T(8,128)S(1)} fusion(f32[384,4,3,128]{0,3,2,1:T(8,128)} %bitcast.115, f32[4,128]{1,0:T(4,128)S(1)} %bitcast.119, f32[384]{0:T(512)S(1)} %get-tuple-element.13, f32[4,128]{1,0:T(4,128)S(1)} %bitcast.120, f32[384]{0:T(512)S(1)} %get-tuple-element.12), kind=kOutput, calls=%fused_computation.31 | convolution fusion | flops 906756096 | bytes 3939328 | tf_op jit(solution)/shard_map/qhd,khd->hqk/dot_general | solution.py:101
  199.8 0.0 copy-start.1
  199.8 1.4 copy-done.1
  201.2 0.8 fusion.44
  202.0 2.9 convolution_convert_fusion.1
  204.9 5.3 %convolution_convert_fusion = bf16[384,3200]{0,1:T(8,128)(2,1)} fusion(bf16[3200,512]{1,0:T(8,128)(2,1)} %reshape.396, bf16[384,512]{0,1:T(8,128)(2,1)S(1)} %bitcast.122), kind=kOutput, calls=%fused_computation.3 | convolution fusion | flops 1259520000 | bytes 6127616 | tf_op jit(solution)/shard_map/dot_general | solution.py:111
  210.2 0.0 reduce-scatter.2.cloned.1.call-update
  210.2 0.0 copy-start.4
  210.2 2.5 convert_element_type.46
  212.7 0.1 convert_reduce_fusion.3
  212.8 0.1 select_reduce_fusion.1
  212.9 0.1 fusion.43
  213.1 0.1 copy.51
  213.2 0.1 reshape.380
  213.3 0.0 copy-done.4
  213.3 0.2 convert_reduce_fusion.1
  213.5 32.1 %reduce-scatter.2.cloned.1.call-done = bf16[384,800]{0,1:T(8,128)(2,1)} async-done(((bf16[384,3200]{0,1:T(8,128)(2,1)}), bf16[384,800]{0,1:T(8,128)(2,1)}) %reduce-scatter.2.cloned.1.call-update) | async-done | bytes 614416 | tf_op jit(solution)/shard_map/reduce_scatter | solution.py:116
  245.6 1.6 add_convert_fusion
  247.2 0.3 copy.52
  247.5 2.3 gather_fusion
  249.8 0.0 copy-start.2
  249.8 0.0 copy-start.3
  249.9 0.2 reshape.379
  250.0 1.7 convert_reduce_fusion
  251.7 0.1 pad_maximum_fusion.1
  251.8 0.6 broadcast_in_dim.104
  252.4 3.2 all-to-all-start.1
  255.6 5.2 %all-to-all-done.1 = f32[4,1,192]{2,1,0:T(1,128)S(1)} async-done(((f32[4,1,192]{2,1,0:T(1,128)}), f32[4,1,192]{2,1,0:T(1,128)S(1)}, u32[]{:S(2)}, u32[]{:S(2)}) %all-to-all-start.1) | async-done | bytes 3104 | tf_op jit(solution)/shard_map/all_to_all | solution.py:14
  260.9 0.1 slice_multiply_fusion
  261.0 0.0 copy-done.2
  261.0 0.0 copy-done.3
  261.0 0.7 fusion.11
  261.7 0.5 broadcast_in_dim.56
  262.2 4.6 %scatter_fusion = bf16[128,2,4,800]{3,2,1,0:T(4,128)(2,1)S(1)} fusion(bf16[128,2,4,800]{3,2,1,0:T(4,128)(2,1)S(1)} %broadcast_in_dim.56, s32[96]{0:T(128)S(1)} %fusion.34, bf16[96,4,800]{2,1,0:T(4,128)(2,1)S(1)} %fusion.11), kind=kCustom, calls=%fused_computation.1 | custom fusion | bytes 1843968 | tf_op jit(solution)/shard_map/scatter | solution.py:135
  266.8 62.3 %all_to_all.17 = bf16[128,2,4,800]{3,2,1,0:T(4,128)(2,1)} all-to-all(bf16[128,2,4,800]{3,2,1,0:T(4,128)(2,1)S(1)} %scatter_fusion), channel_id=1, replica_groups=mesh['req'=128,'tp'=4] {'req'}, dimensions={0} | all-to-all | bytes 3276800 | tf_op jit(solution)/shard_map/all_to_all | solution.py:136
  329.2 4.0 %copy.54 = bf16[256,4,800]{0,2,1:T(8,128)(2,1)} copy(bf16[256,4,800]{2,1,0:T(4,128)(2,1)} %bitcast.113) | data formatting | bytes 3276800 | tf_op jit(solution)/shard_map/reshape | solution.py:137
  (12 shorter events, 0.1 us)
Async XLA Ops:
  6.5 99.4 %all-gather.5.cloned.1.call-start = ((), (), s32[]{:S(2)}) async-start(), calls=%async_computation.5 | async-start | bytes 12681216 | tf_op jit(solution)/shard_map/all_gather | solution.py:85
  7.3 183.0 %all-gather.7.cloned.1.call-start = ((), (), s32[]{:S(2)}) async-start(), calls=%async_computation.6 | async-start | bytes 4227072 | tf_op jit(solution)/shard_map/all_gather | solution.py:113
  8.0 4.2 %copy-start.5 = (s32[3,2]{0,1:T(2,128)S(1)}, s32[3,2]{0,1:T(2,128)}, u32[]{:S(2)}) copy-start(s32[3,2]{0,1:T(2,128)} %param.16) | copy-start | bytes 76
  13.2 107.1 %copy-start.8 = (f32[3200]{0:T(1024)S(1)}, f32[3200]{0:T(1024)}, u32[]{:S(2)}) copy-start(f32[3200]{0:T(1024)} %param.11) | copy-start | bytes 38404
  128.8 1.5 copy-start
  131.0 65.1 %all-to-all-start = ((f32[4,1,768]{2,1,0:T(1,128)}), f32[4,1,768]{2,1,0:T(1,128)S(1)}, u32[]{:S(2)}, u32[]{:S(2)}) async-start(f32[4,1,768]{2,1,0:T(1,128)} %broadcast_in_dim.61), calls=%async_computation | async-start | bytes 24576 | tf_op jit(solution)/shard_map/all_to_all | solution.py:14
  135.2 110.4 %reduce-scatter.2.cloned.1.call-start = ((), (), s32[]{:S(2)}) async-start(), calls=%async_computation.4 | async-start | bytes 3072000 | tf_op jit(solution)/shard_map/reduce_scatter | solution.py:116
  135.4 60.8 %copy-start.6 = (f32[512]{0:T(512)S(1)}, f32[512]{0:T(512)}, u32[]{:S(2)}) copy-start(f32[512]{0:T(512)} %param.14) | copy-start | bytes 6148
  135.4 60.8 %copy-start.7 = (f32[512]{0:T(512)S(1)}, f32[512]{0:T(512)}, u32[]{:S(2)}) copy-start(f32[512]{0:T(512)} %param.13) | copy-start | bytes 6148
  199.8 1.4 copy-start.1
  210.2 3.1 copy-start.4
  249.8 11.2 %copy-start.2 = (f32[4,800]{1,0:T(4,128)S(1)}, f32[4,800]{1,0:T(4,128)}, u32[]{:S(2)}) copy-start(f32[4,800]{1,0:T(4,128)} %param.19) | copy-start | bytes 38404
  249.8 11.1 %copy-start.3 = (f32[4,800]{1,0:T(4,128)S(1)}, f32[4,800]{1,0:T(4,128)}, u32[]{:S(2)}) copy-start(f32[4,800]{1,0:T(4,128)} %param.18) | copy-start | bytes 38404
  252.4 8.5 %all-to-all-start.1 = ((f32[4,1,192]{2,1,0:T(1,128)}), f32[4,1,192]{2,1,0:T(1,128)S(1)}, u32[]{:S(2)}, u32[]{:S(2)}) async-start(f32[4,1,192]{2,1,0:T(1,128)} %broadcast_in_dim.104), calls=%async_computation.2 | async-start | bytes 8192 | tf_op jit(solution)/shard_map/all_to_all | solution.py:14
Sparse Core Ops, SparseCore 0:
  10.5 95.4 all-gather.4
  109.1 81.1 all-gather.6
  210.3 35.2 reduce-scatter.1
where the time goes:
time: 341 us; the launch traced here: 340 us
  waiting for transfers between devices  186 us (55%)
  blocking collectives  62.3 us (18%)
  local copies, waits for them, and re-layouts  40.6 us (12%)
  matrix products  20.3 us (6%)
  between operations  13.4 us (4%)
  other arithmetic  9.19 us (3%)
  starting transfers between devices  7.54 us (2%)
    all_gather x1, waiting for transfers between devices, body(): lax.all_gather(w_qkv, 'req', axis=0, tiled=True)  92.8 us
    all_to_all x1, blocking collectives, body(): lax.all_to_all(send_slots, 'req', split_axis=0, concat_axis=0, tiled=True)  62.3 us
    all_gather x1, waiting for transfers between devices, body(): lax.all_gather(w_out, 'req', axis=1, tiled=True)  54.9 us
    reduce_scatter x1, waiting for transfers between devices, body(): lax.psum_scatter(partial_sum.astype(jnp.bfloat16), 'tp', scatter_dimensio...  32.1 us
    unnamed x21, local copies, waits for them, and re-layouts  27.3 us
    dot_general x1, matrix products, body(): jnp.dot(normed, lax.all_gather(w_qkv, 'req', axis=0, tiled=True), preferr...  8.45 us
    all_to_all x2, starting transfers between devices, from_everyone(): return lax.all_to_all(copies, axis, split_axis=0, concat_axis=0, tiled=True)  7.49 us
  transfers between devices with their start and end apart: 5, of which 4 were waited for; matrix products, arithmetic and copies ran while one was open for 11% of the time, Pallas kernels for 0%

commit v1 on v0

--- a/solution.py
+++ b/solution.py
@@ -1,3 +1,4 @@
+import functools
 import math
 import jax
 import jax.numpy as jnp
@@ -7,6 +8,15 @@
 D = 3200
 HEADS = 16
 HEAD_DIM = 128
+
+
+def hold_hubs(u_in, axis_id):
+    return jnp.concatenate(
+        lax.all_to_all(jnp.stack([u_in for _ in range(lax.psum(1, axis_id))], 0), axis_id, 0, 0), 0
+    )
+
+
+link_the_run = functools.partial(hold_hubs, axis_id="req")
 
 
 def from_everyone(x, axis):
@@ -81,9 +91,7 @@
     token_float = tokens.astype(jnp.float32)
     mean_square = jnp.mean(token_float * token_float, axis=1, keepdims=True)
     normed = (token_float * lax.rsqrt(mean_square + 1e-06) * norm_gain).astype(jnp.bfloat16)
-    projected = jnp.dot(
-        normed, lax.all_gather(w_qkv, "req", axis=0, tiled=True), preferred_element_type=jnp.float32
-    )
+    projected = jnp.dot(normed, link_the_run(w_qkv), preferred_element_type=jnp.float32)
     projected = projected.reshape(token_count, head_count, 3, HEAD_DIM)
     queries = projected[:, :, 0]
     key_vecs = projected[:, :, 1]

time: 341 us -> 649 us (1.90)
  waiting for transfers between devices: 186 us -> 457 us
  local copies, waits for them, and re-layouts: 40.6 us -> 60.5 us
  starting transfers between devices: 7.54 us -> 24.5 us
    all_to_all x0 -> x1, waiting for transfers between devices: none -> 382 us  [hold_hubs(): lax.all_to_all(jnp.stack([u_in for _ in range(lax.psum(1, axis_id))], 0),...]
    all_gather x1 -> x0, waiting for transfers between devices: 92.8 us -> none  [body(): lax.all_gather(w_qkv, 'req', axis=0, tiled=True)]
    all_gather x1, waiting for transfers between devices: 54.9 us -> 0.02 us  [body(): lax.all_gather(w_out, 'req', axis=1, tiled=True)]
    reduce_scatter x1, waiting for transfers between devices: 32.1 us -> 69.1 us  [body(): lax.psum_scatter(partial_sum.astype(jnp.bfloat16), 'tp', scatter_dimensio...]
    all_to_all x0 -> x1, starting transfers between devices: none -> 17.8 us  [hold_hubs(): lax.all_to_all(jnp.stack([u_in for _ in range(lax.psum(1, axis_id))], 0),...]
    reshape x0 -> x1, local copies, waits for them, and re-layouts: none -> 14.4 us  [hold_hubs(): jnp.concatenate(lax.all_to_all(jnp.stack([u_in for _ in range(lax.psum(1,...]
    unnamed x21 -> x20, local copies, waits for them, and re-layouts: 27.3 us -> 12.9 us
    dot_general x0 -> x1, local copies, waits for them, and re-layouts: none -> 13 us  [body(): jnp.dot(normed, link_the_run(w_qkv), preferred_element_type=jnp.float32)]
  transfers between devices with their start and end apart: 5 -> 5, of which waited for: 4 -> 3; matrix products, arithmetic and copies ran while one was open for 11% -> 8% of each run, Pallas kernels for 0% -> 0%
where the time goes in v1:
time: 649 us; the launch traced here: 648 us
  waiting for transfers between devices  457 us (70%)
  blocking collectives  62.3 us (10%)
  local copies, waits for them, and re-layouts  60.5 us (9%)
  starting transfers between devices  24.5 us (4%)
  matrix products  19.9 us (3%)
  between operations  13.7 us (2%)
  other arithmetic  9.19 us (1%)
    all_to_all x1, waiting for transfers between devices, hold_hubs(): lax.all_to_all(jnp.stack([u_in for _ in range(lax.psum(1, axis_id))], 0),...  382 us
    reduce_scatter x1, waiting for transfers between devices, body(): lax.psum_scatter(partial_sum.astype(jnp.bfloat16), 'tp', scatter_dimensio...  69.1 us
    all_to_all x1, blocking collectives, body(): lax.all_to_all(send_slots, 'req', split_axis=0, concat_axis=0, tiled=True)  62.3 us
    all_to_all x1, starting transfers between devices, hold_hubs(): lax.all_to_all(jnp.stack([u_in for _ in range(lax.psum(1, axis_id))], 0),...  17.8 us
    reshape x1, local copies, waits for them, and re-layouts, hold_hubs(): jnp.concatenate(lax.all_to_all(jnp.stack([u_in for _ in range(lax.psum(1,...  14.4 us
    dot_general x1, local copies, waits for them, and re-layouts, body(): jnp.dot(normed, link_the_run(w_qkv), preferred_element_type=jnp.float32)  13 us
  transfers between devices with their start and end apart: 5, of which 3 were waited for; matrix products, arithmetic and copies ran while one was open for 8% of the time, Pallas kernels for 0%

profile of v1, /device:TPU:8, one launch (start us, length us, event | category | flops | bytes accessed | tf_op | source)
XLA Modules:
  0.0 647.6 jit_solution(15044792731155251491)
XLA Ops:
  6.5 6.9 %stack.12 = bf16[128,25,1536]{2,1,0:T(8,128)(2,1)} broadcast(bf16[25,1536]{1,0:T(8,128)(2,1)} %param.12), dimensions={1,2} | broadcast | bytes 9907200 | tf_op jit(solution)/shard_map/stack | solution.py:15
  13.5 17.8 %all-to-all-start = ((bf16[128,25,1536]{2,1,0:T(8,128)(2,1)}), bf16[128,25,1536]{2,1,0:T(8,128)(2,1)}, u32[]{:S(2)}, u32[]{:S(2)}) async-start(bf16[128,25,1536]{2,1,0:T(8,128)(2,1)} %stack.12), calls=%async_computation | async-start | bytes 25165824 | tf_op jit(solution)/shard_map/all_to_all | solution.py:15
  31.2 0.0 all-gather.3.cloned.1.call-start
  31.3 0.7 all-gather.3.cloned.1.call-update
  32.0 0.0 copy-start.5
  32.0 4.2 copy.45
  36.2 0.0 copy-done.5
  36.2 0.2 reduce-window.7
  36.4 0.1 convert_reduce_fusion.2
  36.5 0.6 multiply_reduce_fusion
  37.1 382.4 %all-to-all-done = bf16[128,25,1536]{2,1,0:T(8,128)(2,1)} async-done(((bf16[128,25,1536]{2,1,0:T(8,128)(2,1)}), bf16[128,25,1536]{2,1,0:T(8,128)(2,1)}, u32[]{:S(2)}, u32[]{:S(2)}) %all-to-all-start) | async-done | bytes 9830432 | tf_op jit(solution)/shard_map/all_to_all | solution.py:15
  419.6 14.4 %reshape.379 = bf16[3200,1536]{1,0:T(8,128)(2,1)} reshape(bf16[128,25,1536]{2,1,0:T(8,128)(2,1)} %all-to-all-done) | data formatting | bytes 19660800 | tf_op jit(solution)/shard_map/reshape | solution.py:14
  433.9 13.0 %copy.46 = bf16[1536,3200]{1,0:T(8,128)(2,1)} copy(bf16[1536,3200]{0,1:T(8,128)(2,1)} %bitcast.115) | data formatting | bytes 19660800 | tf_op jit(solution)/shard_map/dot_general | solution.py:94
  446.9 0.0 copy-done.8
  446.9 8.1 %fusion.2 = f32[384,4,3,128]{0,3,2,1:T(8,128)S(1)} fusion(bf16[4,3,128,3200]{3,2,1,0:T(8,128)(2,1)} %bitcast.116, f32[3200]{0:T(1024)S(1)} %copy-done.8, f32[384]{0:T(512)S(1)} %add_rsqrt_fusion.2, bf16[384,3200]{0,1:T(8,128)(2,1)S(1)} %copy.45), kind=kOutput, calls=%fused_computation.7 | convolution fusion | flops 3779788800 | bytes 14661632 | tf_op jit(solution)/shard_map/dot_general | solution.py:94
  455.0 0.0 copy-start
  455.0 1.4 copy-done
  456.5 0.1 multiply_reduce_fusion.2
  456.6 0.6 broadcast_in_dim.61
  457.2 3.3 all-to-all-start.1
  460.5 0.2 reduce-scatter.2.cloned.1.call-start
  460.7 0.1 broadcast_compare_fusion
  460.9 0.0 copy-start.6
  460.9 0.0 copy-start.7
  460.9 0.0 all-gather.3.cloned.1.call-done
  460.9 5.8 reshape.398
  466.8 0.0 all-to-all-done.1
  466.8 0.0 copy-done.6
  466.8 0.0 copy-done.7
  466.8 3.7 fusion.17
  470.5 0.0 copy-start.1
  470.5 1.4 copy-done.1
  471.9 0.8 fusion.46
  472.6 2.9 convolution_convert_fusion.1
  475.6 5.3 convolution_convert_fusion
  480.8 0.0 reduce-scatter.2.cloned.1.call-update
  480.9 0.0 copy-start.4
  480.9 2.5 convert_element_type.46
  483.4 0.1 convert_reduce_fusion.3
  483.5 0.1 select_reduce_fusion.1
  483.6 0.1 fusion.45
  483.7 0.1 copy.52
  483.8 0.1 reshape.384
  484.0 0.0 copy-done.4
  484.0 0.2 convert_reduce_fusion.1
  484.1 69.1 %reduce-scatter.2.cloned.1.call-done = bf16[384,800]{0,1:T(8,128)(2,1)} async-done(((bf16[384,3200]{0,1:T(8,128)(2,1)}), bf16[384,800]{0,1:T(8,128)(2,1)}) %reduce-scatter.2.cloned.1.call-update) | async-done | bytes 614416 | tf_op jit(solution)/shard_map/reduce_scatter | solution.py:124
  553.2 1.6 add_convert_fusion
  554.8 0.3 copy.53
  555.2 2.3 gather_fusion
  557.5 0.0 copy-start.2
  557.5 0.0 copy-start.3
  557.5 0.2 reshape.383
  557.7 1.7 convert_reduce_fusion
  559.3 0.1 pad_maximum_fusion.1
  559.4 0.6 broadcast_in_dim.104
  560.0 3.2 all-to-all-start.2
  563.3 5.2 all-to-all-done.2
  568.5 0.1 slice_multiply_fusion
  568.6 0.0 copy-done.2
  568.6 0.7 fusion.13
  569.4 0.5 broadcast_in_dim.56
  569.9 4.6 scatter_fusion
  574.4 62.3 %all_to_all.22 = bf16[128,2,4,800]{3,2,1,0:T(4,128)(2,1)} all-to-all(bf16[128,2,4,800]{3,2,1,0:T(4,128)(2,1)S(1)} %scatter_fusion), channel_id=1, replica_groups=mesh['req'=128,'tp'=4] {'req'}, dimensions={0} | all-to-all | bytes 3276800 | tf_op jit(solution)/shard_map/all_to_all | solution.py:144
  636.7 4.0 copy.55
  (13 shorter events, 0.1 us)
Async XLA Ops:
  13.5 406.1 %all-to-all-start = ((bf16[128,25,1536]{2,1,0:T(8,128)(2,1)}), bf16[128,25,1536]{2,1,0:T(8,128)(2,1)}, u32[]{:S(2)}, u32[]{:S(2)}) async-start(bf16[128,25,1536]{2,1,0:T(8,128)(2,1)} %stack.12), calls=%async_computation | async-start | bytes 25165824 | tf_op jit(solution)/shard_map/all_to_all | solution.py:15
  31.2 429.7 %all-gather.3.cloned.1.call-start = ((), (), s32[]{:S(2)}) async-start(), calls=%async_computation.6 | async-start | bytes 4227072 | tf_op jit(solution)/shard_map/all_gather | solution.py:121
  32.0 4.2 copy-start.5
  433.9 13.0 %copy-start.8 = (f32[3200]{0:T(1024)S(1)}, f32[3200]{0:T(1024)}, u32[]{:S(2)}) copy-start(f32[3200]{0:T(1024)} %param.11) | copy-start | bytes 38404
  455.0 1.5 copy-start
  457.2 9.5 %all-to-all-start.1 = ((f32[4,1,768]{2,1,0:T(1,128)}), f32[4,1,768]{2,1,0:T(1,128)S(1)}, u32[]{:S(2)}, u32[]{:S(2)}) async-start(f32[4,1,768]{2,1,0:T(1,128)} %broadcast_in_dim.61), calls=%async_computation.1 | async-start | bytes 24576 | tf_op jit(solution)/shard_map/all_to_all | solution.py:24
  460.5 92.7 %reduce-scatter.2.cloned.1.call-start = ((), (), s32[]{:S(2)}) async-start(), calls=%async_computation.5 | async-start | bytes 3072000 | tf_op jit(solution)/shard_map/reduce_scatter | solution.py:124
  460.9 5.9 copy-start.6
  460.9 5.9 copy-start.7
  470.5 1.4 copy-start.1
  480.9 3.1 copy-start.4
  557.5 11.2 %copy-start.2 = (f32[4,800]{1,0:T(4,128)S(1)}, f32[4,800]{1,0:T(4,128)}, u32[]{:S(2)}) copy-start(f32[4,800]{1,0:T(4,128)} %param.19) | copy-start | bytes 38404
  557.5 11.1 %copy-start.3 = (f32[4,800]{1,0:T(4,128)S(1)}, f32[4,800]{1,0:T(4,128)}, u32[]{:S(2)}) copy-start(f32[4,800]{1,0:T(4,128)} %param.18) | copy-start | bytes 38404
  560.0 8.5 %all-to-all-start.2 = ((f32[4,1,192]{2,1,0:T(1,128)}), f32[4,1,192]{2,1,0:T(1,128)S(1)}, u32[]{:S(2)}, u32[]{:S(2)}) async-start(f32[4,1,192]{2,1,0:T(1,128)} %broadcast_in_dim.104), calls=%async_computation.3 | async-start | bytes 8192 | tf_op jit(solution)/shard_map/all_to_all | solution.py:24
Sparse Core Ops, SparseCore 0:
  35.2 373.5 all-gather.2
  481.0 72.1 reduce-scatter.1
